TPU v7x, 32 devices: a whole 2x2x4 slice. The times are simulated.
32 devices in a mesh: ew: 8 (over y, x, core), ns: 4 (over z).
Axes of the slice: x: 2, y: 2, z: 4, core: 2. Of those that a mesh axis runs over, the one named last changes fastest.
Arguments:
- fluid: float32 [19, 32, 64, 1024], P(None, None, 'ew', 'ns'), may hold values from 0 to 0.6, as said below
- heat: float32 [7, 32, 64, 1024], P(None, None, 'ew', 'ns'), may hold values from 0 to 0.4, as said below
- solid_mask: int32 [32, 64, 1024], P(None, 'ew', 'ns'), may hold values 0 or 1
- inflow_type: int32 [32, 1024], P(None, 'ns'), may hold values from 0 to 2
Outputs:
- fluid_next: float32 [19, 32, 64, 1024], P(None, None, 'ew', 'ns')
- heat_next: float32 [7, 32, 64, 1024], P(None, None, 'ew', 'ns')
Inputs may be any that keep to these rules, and one draw needn't show every extreme that they name: `fluid`: each population is positive. `heat`: each population is positive.
All inputs are finite; a program needn't handle non-finite values. No bound on the sum of `solid_mask` on one device may be relied on, other than what follows from the above.
Results may differ from a plain program's by a relative error of at most 0.0001.
Values sent between devices are 32-bit elements; how exact they have to be, the bound alone decides.
No kernel may reach another device: no remote copies, remote signals or barrier semaphores. Data moves between devices by JAX's collectives and lax.ppermute only.
A program may use at most 192 MiB of HBM per device.

v0:
```python
import functools
import math

import jax
import jax.numpy as jnp
from jax import lax
from jax.experimental import pallas as pl
from jax.experimental.pallas import tpu as pltpu
from jax.sharding import PartitionSpec as P

FLUID_DIRS = [
    (0, 0, 0),
    (1, 0, 0),
    (-1, 0, 0),
    (0, 1, 0),
    (0, -1, 0),
    (0, 0, 1),
    (0, 0, -1),
    (1, 1, 0),
    (-1, -1, 0),
    (1, -1, 0),
    (-1, 1, 0),
    (1, 0, 1),
    (-1, 0, -1),
    (1, 0, -1),
    (-1, 0, 1),
    (0, 1, 1),
    (0, -1, -1),
    (0, 1, -1),
    (0, -1, 1),
]
DIRS = FLUID_DIRS + FLUID_DIRS[:7]
NF, NH = 19, 7
NP = NF + NH
OPP = [
    (FLUID_DIRS.index((-c[0], -c[1], -c[2])) + (0 if i < NF else NF)) for i, c in enumerate(DIRS)
]
WEIGHTS = (
    [1.0 / 3.0] + [1.0 / 18.0] * 6 + [1.0 / 36.0] * 12 + [0.25] + [0.125] * 6
)
PLUS = [i for i, c in enumerate(DIRS) if c[0] == 1]
MINUS = [i for i, c in enumerate(DIRS) if c[0] == -1]
TAU = 0.6
TAU_HEAT = 0.8
COUPLING = 0.02
INFLOW_SPEED = 0.08
COOLING = 0.2
MARK = float("nan")
MASK, KIND = NP, NP + 1
SLOTS = NP + 2
NMOVE = len(PLUS)
NFACE = NMOVE + 1
TILE = 128
GROUP = 4
GROUPS = SLOTS // GROUP
PITCH = TILE // GROUP


def collided(f, solid):
    pairs = {k: (f[k] + f[k + 1], f[k] - f[k + 1]) for k in range(1, NF, 2)}
    s = {k: v[0] for k, v in pairs.items()}
    d = {k: v[1] for k, v in pairs.items()}
    rho = (f[0] + (s[1] + s[3])) + ((s[5] + s[7]) + (s[9] + s[11])) + ((s[13] + s[15]) + s[17])
    mx = (d[1] + d[7]) + (d[9] + (d[11] + d[13]))
    my = (d[3] + d[7]) + ((d[15] - d[9]) + d[17])
    mz = (d[5] + d[11]) + ((d[15] - d[13]) - d[17])
    g = f[NF:]
    hp = [(g[k] + g[k + 1]) for k in (1, 3, 5)]
    warm = (g[0] + hp[0]) + (hp[1] + hp[2])
    inv = 1.0 / rho
    ux, uy, uz = mx * inv, my * inv, mz * inv
    lifted = uz + TAU * COUPLING * (warm - 1.0)
    root = math.sqrt(4.5)
    ax, ay, az = ux * root, uy * root, lifted * root
    base = 1.0 - (ax * ax + ay * ay + az * az) * (1.0 / 3.0)
    keep = 1.0 - 1.0 / TAU
    r = jnp.where(solid, MARK, rho * (1.0 / TAU))
    r18, r36 = r * (1.0 / 18.0), r * (1.0 / 36.0)
    o18, o36 = r18 * (3.0 / root), r36 * (3.0 / root)
    out = [None] * NP
    out[0] = keep * f[0] + (r * (1.0 / 3.0)) * base
    along = {
        1: ax,
        3: ay,
        5: az,
        7: ax + ay,
        9: ax - ay,
        11: ax + az,
        13: ax - az,
        15: ay + az,
        17: ay - az,
    }
    for k, e in along.items():
        w, o = (r18, o18) if k < 7 else (r36, o36)
        even = w * (base + e * e)
        odd = o * e
        out[k] = keep * f[k] + (even + odd)
        out[k + 1] = keep * f[k + 1] + (even - odd)
    hkeep = 1.0 - 1.0 / TAU_HEAT
    t8 = jnp.where(solid, MARK, warm * (0.125 / TAU_HEAT))
    out[NF] = hkeep * g[0] + (t8 + t8)
    t2 = t8 * 4.0
    for k, u in ((1, ux), (3, uy), (5, uz)):
        odd = t2 * u
        out[NF + k] = hkeep * g[k] + (t8 + odd)
        out[NF + k + 1] = hkeep * g[k + 1] + (t8 - odd)
    return out


def ghost(i, kind):
    u = (INFLOW_SPEED * 0.5) * kind
    cx = DIRS[i][0]
    if i < NF:
        return WEIGHTS[i] * (1.0 + 3.0 * cx * u + (4.5 * cx * cx - 1.5) * (u * u))
    return WEIGHTS[i] * (1.0 - COOLING * kind) * (1.0 + 4.0 * cx * u)


def marked(v):
    return v != v


def clean(v):
    return jnp.where(marked(v), 0.0, v)


def collide_kernel(tiles, *refs):
    fluid, heat, mask = refs[:tiles], refs[tiles : 2 * tiles], refs[2 * tiles : 3 * tiles]
    post, west, east = refs[3 * tiles :]
    width, rows = post.shape[0], post.shape[2]

    def column(x, carry):
        cells = pl.ds(x, rows, stride=width)
        for t in range(tiles):
            span = pl.ds(t * TILE, TILE)
            f = [fluid[t][i, cells] for i in range(NF)]
            f += [heat[t][i, cells] for i in range(NH)]
            for i, v in enumerate(collided(f, mask[t][cells] > 0)):
                post[x, i, :, span] = v
        return carry

    lax.fori_loop(0, width, column, 0)

    for face, near, moving in ((west, 0, MINUS), (east, width - 1, PLUS)):
        for t in range(tiles):
            span = pl.ds(t * TILE, TILE)
            for n, i in enumerate(moving):
                face[n * tiles + t] = clean(post[near, i, :, span])
            face[NMOVE * tiles + t] = jnp.where(marked(post[near, 0, :, span]), 1.0, 0.0)


def column_kernel(width, *refs):
    fluid, heat, mask, kind, packed = refs[:2], refs[2:4], refs[4:6], refs[6:8], refs[8]
    rows = packed.shape[1]
    lanes = lax.broadcasted_iota(jnp.int32, (rows, TILE), 1)
    start, stop = lanes < 2, lanes >= TILE - 2

    def ends(pair, x):
        a, b = (v.astype(jnp.float32) for v in pair)
        both = jnp.where(stop, b, jnp.where(start, a, 0.0))
        return pltpu.roll(both, (x * 4 + 2) % TILE, 1)

    def gathered(read):
        total = ends(read(0), 0)
        for x in range(1, width):
            total = total + ends(read(x), x)
        return total

    def cells(x):
        return pl.ds(x, rows, stride=width)

    f = [gathered(lambda x: [r[i, cells(x)] for r in fluid]) for i in range(NF)]
    f += [gathered(lambda x: [r[i, cells(x)] for r in heat]) for i in range(NH)]
    solid = gathered(lambda x: [r[cells(x)] for r in mask])
    idle = (solid > 0.5) | (lanes >= 4 * width)
    out = [jnp.where(idle, 0.0, v) for v in collided(f, solid > 0.5)]
    out += [solid, gathered(lambda x: [r[...] for r in kind])]
    for group in range(GROUPS):
        total = out[group * GROUP]
        for k in range(1, GROUP):
            total = total + pltpu.roll(out[group * GROUP + k], k * PITCH, 1)
        packed[group] = total


def column_call(fluid, heat, mask, kind):
    depth, width, length = mask.shape
    rows = 8
    block = rows * width
    ends = (0, length // TILE - 1)
    return pl.pallas_call(
        functools.partial(column_kernel, width),
        grid=(depth // rows,),
        in_specs=[pl.BlockSpec((NF, block, TILE), lambda z, t=t: (0, z, t)) for t in ends]
        + [pl.BlockSpec((NH, block, TILE), lambda z, t=t: (0, z, t)) for t in ends]
        + [pl.BlockSpec((block, TILE), lambda z, t=t: (z, t)) for t in ends]
        + [pl.BlockSpec((rows, TILE), lambda z, t=t: (z, t)) for t in ends],
        out_specs=pl.BlockSpec((GROUPS, rows, TILE), lambda z: (0, z, 0)),
        out_shape=jax.ShapeDtypeStruct((GROUPS, depth, TILE), jnp.float32),
        cost_estimate=cost(depth * width * length, 2),
        compiler_params=pltpu.CompilerParams(vmem_limit_bytes=12 * 2**20),
        name="columns",
    )(
        *[in_hbm(fluid.reshape(NF, depth * width, length))] * 2,
        *[in_hbm(heat.reshape(NH, depth * width, length))] * 2,
        *[in_hbm(mask.reshape(depth * width, length))] * 2,
        *[kind] * 2,
    )


def in_hbm(v):
    return pltpu.with_memory_space_constraint(v, pltpu.HBM)


def cost(cells, passes):
    return pl.CostEstimate(
        flops=300 * cells * passes, bytes_accessed=4 * NP * cells * passes, transcendentals=0
    )


def collide_call(fluid, heat, mask):
    depth, width, length = mask.shape
    rows = 8
    block = rows * width
    f32 = jnp.float32
    tiles = length // TILE
    span = range(tiles)
    return pl.pallas_call(
        functools.partial(collide_kernel, tiles),
        grid=(depth // rows,),
        in_specs=[pl.BlockSpec((NF, block, TILE), lambda z, t=t: (0, z, t)) for t in span]
        + [pl.BlockSpec((NH, block, TILE), lambda z, t=t: (0, z, t)) for t in span]
        + [pl.BlockSpec((block, TILE), lambda z, t=t: (z, t)) for t in span],
        out_specs=[
            pl.BlockSpec((width, NP, rows, length), lambda z: (0, 0, z, 0)),
            pl.BlockSpec((NFACE * tiles, rows, TILE), lambda z: (0, z, 0)),
            pl.BlockSpec((NFACE * tiles, rows, TILE), lambda z: (0, z, 0)),
        ],
        out_shape=[
            jax.ShapeDtypeStruct((width, NP, depth, length), f32),
            jax.ShapeDtypeStruct((NFACE * tiles, depth, TILE), f32),
            jax.ShapeDtypeStruct((NFACE * tiles, depth, TILE), f32),
        ],
        cost_estimate=cost(depth * width * length, 2),
        compiler_params=pltpu.CompilerParams(vmem_limit_bytes=16 * 2**20),
        name="collide",
    )(
        *[in_hbm(fluid.reshape(NF, depth * width, length))] * tiles,
        *[in_hbm(heat.reshape(NH, depth * width, length))] * tiles,
        *[in_hbm(mask.reshape(depth * width, length))] * tiles,
    )


class Lanes:
    def __init__(self, depth, width, place):
        shape = (depth, TILE)
        lane = lax.broadcasted_iota(jnp.int32, shape, 1)
        level = lax.broadcasted_iota(jnp.int32, shape, 0)
        self.side, self.slot, self.j = lane // 64, (lane % 64) // 4, lane % 4
        self.ground, self.top = level == 0, level == depth - 1
        self.first, self.last = lane == 0, lane == TILE - 1
        self.west, self.east = place[0] == 1, place[1] == 1
        low = (place[2] == 1) & (self.side == 0) & (self.j < 2)
        high = (place[3] == 1) & (self.side == 1) & (self.j >= 2)
        self.beyond_y = low | high


def strip_kernel(width, place, own, even, odd, west, east, strip, to_west, to_east):
    depth = own.shape[1]
    at = Lanes(depth, width, place)
    flip = place[4] == 1
    slots_w = [None] * NFACE
    slots_e = [None] * NFACE
    near_j = at.j < 2
    for group in range(GROUPS):
        o = own[group]
        above = jnp.where(flip, odd[group], even[group])
        below = jnp.where(flip, even[group], odd[group])
        low, high = jnp.where(near_j, below, o), jnp.where(near_j, o, above)
        for k in range(GROUP):
            p = group * GROUP + k
            v = jnp.where(
                at.side == 0,
                pltpu.roll(low, (16 - k * PITCH) % TILE, 1),
                pltpu.roll(high, (80 - k * PITCH) % TILE, 1),
            )
            strip[p] = v
            if p in MINUS or p == MASK:
                n = NMOVE if p == MASK else MINUS.index(p)
                slots_w[n] = pltpu.roll(v, (4 * n - 16) % TILE, 1)
            if p in PLUS or p == MASK:
                n = NMOVE if p == MASK else PLUS.index(p)
                slots_e[n] = pltpu.roll(v, (4 * n - 12 - 4 * width) % TILE, 1)
    for out, face, slots in ((to_west, west, slots_w), (to_east, east, slots_e)):
        for n in range(face.shape[0]):
            out[n] = face[n]
        total = jnp.zeros_like(slots[0])
        for n, v in enumerate(slots):
            total = jnp.where(at.slot == n, v, total)
        out[face.shape[0]] = total
    solid = strip[MASK] > 0.5
    for i in range(NP):
        strip[i] = jnp.where(at.beyond_y, WEIGHTS[i], jnp.where(solid, MARK, strip[i]))


def strip_call(width, place, own, even, odd, west, east):
    _, depth, _ = own.shape
    f32 = jnp.float32
    vmem = pl.BlockSpec(memory_space=pltpu.VMEM)
    return pl.pallas_call(
        functools.partial(strip_kernel, width),
        in_specs=[pl.BlockSpec(memory_space=pltpu.SMEM)] + [vmem] * 5,
        out_specs=[vmem, vmem, vmem],
        out_shape=[
            jax.ShapeDtypeStruct((SLOTS, depth, TILE), f32),
            jax.ShapeDtypeStruct((west.shape[0] + 1, depth, TILE), f32),
            jax.ShapeDtypeStruct((west.shape[0] + 1, depth, TILE), f32),
        ],
        compiler_params=pltpu.CompilerParams(vmem_limit_bytes=8 * 2**20),
        name="strips",
    )(place, own, even, odd, west, east)


def raised(v, i, at):
    depth = v.shape[0]
    cz = DIRS[i][2]
    if cz == 1:
        return jnp.where(at.ground, MARK, pltpu.roll(v, 1, 0))
    if cz == -1:
        return jnp.where(at.top, WEIGHTS[i], pltpu.roll(v, depth - 1, 0))
    return v


def pieces(ref, index, i, tiles):
    return [ref[index, i, :, pl.ds(t * TILE, TILE)] for t in range(tiles)]


def pulled(cells, cols, x, i, at):
    cx, cy, _ = DIRS[i]
    source = cells(x - cx, i)
    if cy:
        turned = [pltpu.roll(v, cy % TILE, 1) for v in source]
        lane = (x - cx + 4) * 4
        if cy == 1:
            col = pltpu.roll(cols[i], lax.rem(2 * TILE - (lane + 1), TILE), 1)
            before = [col] + turned[:-1]
            source = [jnp.where(at.first, p, v) for p, v in zip(before, turned)]
        else:
            col = pltpu.roll(cols[i], lax.rem(2 * TILE - 1 - (64 + lane + 2), TILE), 1)
            after = turned[1:] + [col]
            source = [jnp.where(at.last, n, v) for n, v in zip(after, turned)]
    return [raised(v, i, at) for v in source]


def close_strip(strip, kinds, from_west, from_east, solid, at, width):
    kind = jnp.where(at.beyond_y, 0.0, kinds)
    for face, edge, slot, moving in (
        (from_west, at.west, 3, PLUS),
        (from_east, at.east, 4 + width, MINUS),
    ):
        here = at.slot == slot
        for n, i in enumerate(moving):
            v = pltpu.roll(face, (4 * slot - 4 * n) % TILE, 1)
            v = jnp.where(solid, MARK, v)
            v = jnp.where(at.beyond_y, WEIGHTS[i], v)
            v = jnp.where(edge, ghost(i, kind) if slot == 3 else WEIGHTS[i], v)
            strip[i] = jnp.where(here, v, strip[i])


def advance_slab(a, x, near, strip, fresh, out, at):
    depth, length = fresh.shape[1], fresh.shape[2]
    tiles = length // TILE
    for i in range(NP):
        vs = pulled(lambda s, p: pieces(a, s - x + near, p, tiles), strip, x, i, at)
        backs = pieces(a, near, OPP[i], tiles)
        for t, (v, back) in enumerate(zip(vs, backs)):
            fresh[i, :, pl.ds(t * TILE, TILE)] = jnp.where(marked(v), back, v)
    for z in range(0, depth, 8):
        for t in range(tiles):
            part, span = pl.ds(z, 8), pl.ds(t * TILE, TILE)
            f = [fresh[i, part, span] for i in range(NP)]
            solid = marked(a[near, 0, part, span])
            for i, v in enumerate(collided(f, solid)):
                out[i, part, span] = v


def advance_inner_kernel(place, post, strip, next_out, a, fresh, b, load_sem, out_sem):
    width, depth = post.shape[0], post.shape[2]

    def load(x):
        return pltpu.make_async_copy(post.at[x], a.at[x], load_sem.at[x])

    def store(x):
        return pltpu.make_async_copy(b.at[x], next_out.at[x], out_sem.at[x])

    for x in range(width):
        load(x).start()
    at = Lanes(depth, width, place)
    load(0).wait()
    load(1).wait()

    def advance(x, carry):
        load(x + 1).wait()
        advance_slab(a, x, x, strip, fresh, b.at[x], at)
        store(x).start()
        return carry

    lax.fori_loop(1, width - 1, advance, 0)
    for x in range(1, width - 1):
        store(x).wait()


def advance_inner_call(place, post, strip):
    width, _, depth, length = post.shape
    f32 = jnp.float32
    vmem = pl.BlockSpec(memory_space=pltpu.VMEM)
    hbm = pl.BlockSpec(memory_space=pl.ANY)
    return pl.pallas_call(
        advance_inner_kernel,
        in_specs=[pl.BlockSpec(memory_space=pltpu.SMEM), hbm, vmem],
        out_specs=hbm,
        out_shape=jax.ShapeDtypeStruct((width, NP, depth, length), f32),
        scratch_shapes=[
            pltpu.VMEM((width, NP, depth, length), f32),
            pltpu.VMEM((NP, depth, length), f32),
            pltpu.VMEM((width, NP, depth, length), f32),
            pltpu.SemaphoreType.DMA((width,)),
            pltpu.SemaphoreType.DMA((width,)),
        ],
        cost_estimate=cost(depth * width * length, 2),
        compiler_params=pltpu.CompilerParams(vmem_limit_bytes=24 * 2**20),
        name="advance_inner",
    )(place, post, strip)


def ends_of(width):
    return ((0, 1), (1, 2), (width - 2, 3), (width - 1, 4))


def advance_kernel(
    place,
    post,
    west,
    east,
    strip_in,
    kind,
    next_in,
    next_out,
    strip2,
    to_west,
    to_east,
    halo,
    a,
    strip,
    fresh,
    b,
    load_sem,
    out_sem,
):
    width, depth, length = post.shape[0], post.shape[2], post.shape[3]
    tiles = length // TILE
    loads = [
        pltpu.make_async_copy(post.at[x], a.at[n], load_sem.at[n]) for x, n in ends_of(width)
    ]
    for copy in loads:
        copy.start()
    at = Lanes(depth, width, place)
    for p in range(SLOTS):
        strip[p] = strip_in[p]
    ends_w, ends_e = west[NFACE * tiles], east[NFACE * tiles]
    ends = jnp.where(
        at.slot == 3,
        pltpu.roll(ends_w, (12 - 4 * NMOVE) % TILE, 1),
        pltpu.roll(ends_e, (16 + 4 * width - 4 * NMOVE) % TILE, 1),
    )
    kind_end = pltpu.roll(strip[KIND], TILE - 4, 1)
    close_strip(strip, kind_end, ends_w, ends_e, ends > 0.5, at, width)
    halo[0], halo[1] = ends, kind_end
    for n, face in ((2, west), (2 + tiles, east)):
        for t in range(tiles):
            halo[n + t] = face[NMOVE * tiles + t]
    kinds = kind[...].astype(jnp.float32)
    close_faces(a, west, east, halo, kinds, at)

    for i in range(NP):
        cx, cy, _ = DIRS[i]
        v = strip[i]
        if cx or cy:
            v = pltpu.roll(v, (4 * cx + cy) % TILE, 1)
        v = raised(v, i, at)
        fresh[i, :, pl.ds(0, TILE)] = jnp.where(marked(v), strip[OPP[i]], v)
    for z in range(0, depth, 8):
        part = pl.ds(z, 8)
        f = [fresh[i, part, pl.ds(0, TILE)] for i in range(NP)]
        outside = at.beyond_y[z : z + 8]
        for i, v in enumerate(collided(f, marked(strip[0, part]))):
            strip2[i, part] = jnp.where(outside, WEIGHTS[i], v)

    for copy in loads:
        copy.wait()

    def advance(n, carry):
        x = n * (width - 1)
        advance_slab(a, x, 1 + 3 * n, strip, fresh, b.at[n], at)
        pltpu.make_async_copy(b.at[n], next_out.at[x], out_sem.at[n]).start()
        return carry

    lax.fori_loop(0, 2, advance, 0)
    for out, end, near, moving in ((to_west, 0, 0, MINUS), (to_east, 1, width - 1, PLUS)):
        slots = None
        for n, i in enumerate(moving):
            for t in range(tiles):
                out[n * tiles + t] = clean(b[end, i, :, pl.ds(t * TILE, TILE)])
            v = pltpu.roll(clean(strip2[i]), (4 * n - 4 * (near + 4)) % TILE, 1)
            slots = v if slots is None else jnp.where(at.slot == n, v, slots)
        out[NMOVE * tiles] = slots
    for n in range(2):
        pltpu.make_async_copy(b.at[n], next_out.at[n * (width - 1)], out_sem.at[n]).wait()


def advance_call(place, post, west, east, strip, kind, inner):
    width, _, depth, length = post.shape
    tiles = length // TILE
    f32 = jnp.float32
    vmem = pl.BlockSpec(memory_space=pltpu.VMEM)
    hbm = pl.BlockSpec(memory_space=pl.ANY)
    sends = NMOVE * tiles + 1
    return pl.pallas_call(
        advance_kernel,
        in_specs=[pl.BlockSpec(memory_space=pltpu.SMEM), hbm] + [vmem] * 4 + [hbm],
        out_specs=[hbm, vmem, vmem, vmem, vmem],
        out_shape=[
            jax.ShapeDtypeStruct((width, NP, depth, length), f32),
            jax.ShapeDtypeStruct((NP, depth, TILE), f32),
            jax.ShapeDtypeStruct((sends, depth, TILE), f32),
            jax.ShapeDtypeStruct((sends, depth, TILE), f32),
            jax.ShapeDtypeStruct((2 + 2 * tiles, depth, TILE), f32),
        ],
        scratch_shapes=[
            pltpu.VMEM((6, NP, depth, length), f32),
            pltpu.VMEM((SLOTS, depth, TILE), f32),
            pltpu.VMEM((NP, depth, length), f32),
            pltpu.VMEM((2, NP, depth, length), f32),
            pltpu.SemaphoreType.DMA((6,)),
            pltpu.SemaphoreType.DMA((2,)),
        ],
        input_output_aliases={6: 0},
        cost_estimate=cost(depth * 2 * length, 3),
        compiler_params=pltpu.CompilerParams(vmem_limit_bytes=24 * 2**20),
        name="advance",
    )(place, post, west, east, strip, kind, inner)


def close_faces(a, west, east, halo, kinds, at):
    tiles = a.shape[3] // TILE
    for face, edge, near, moving in (
        (west, at.west, 0, PLUS),
        (east, at.east, a.shape[0] - 1, MINUS),
    ):
        for t in range(tiles):
            solid = halo[2 + t if near == 0 else 2 + tiles + t] > 0.5
            span = slice(t * TILE, (t + 1) * TILE)
            for n, i in enumerate(moving):
                v = jnp.where(solid, MARK, face[n * tiles + t])
                outer = ghost(i, kinds[:, span]) if near == 0 else WEIGHTS[i]
                a[near, i, :, span] = jnp.where(edge, outer, v)


def settle_slab(b, x, near, strip, fout, hout, at):
    tiles = b.shape[3] // TILE
    solids = [marked(v) for v in pieces(b, near, 0, tiles)]
    for i in range(NP):
        buffer, index = (fout, i) if i < NF else (hout, i - NF)
        vs = pulled(lambda s, p: pieces(b, s - x + near, p, tiles), strip, x, i, at)
        backs = pieces(b, near, OPP[i], tiles)
        for t, (v, back) in enumerate(zip(vs, backs)):
            span = pl.ds(t * TILE, TILE)
            v = jnp.where(marked(v), back, v)
            buffer[index, :, span] = jnp.where(solids[t], buffer[index, :, span], v)


def settle_inner_kernel(
    place, fluid, heat, post, strip, fluid_out, heat_out, b, fout, hout, load_sem, fill_sem, out_sem
):
    width, depth = post.shape[0], post.shape[2]

    def load(x):
        return pltpu.make_async_copy(post.at[x], b.at[x], load_sem.at[x])

    def fill(x):
        return (
            pltpu.make_async_copy(fluid.at[:, :, x], fout.at[x], fill_sem.at[0, x]),
            pltpu.make_async_copy(heat.at[:, :, x], hout.at[x], fill_sem.at[1, x]),
        )

    def store(x):
        return (
            pltpu.make_async_copy(fout.at[x], fluid_out.at[:, :, x], out_sem.at[0, x]),
            pltpu.make_async_copy(hout.at[x], heat_out.at[:, :, x], out_sem.at[1, x]),
        )

    for x in range(width):
        load(x).start()
        if 0 < x < width - 1:
            for copy in fill(x):
                copy.start()
    at = Lanes(depth, width, place)
    load(0).wait()
    load(1).wait()

    def settle(x, carry):
        load(x + 1).wait()
        for copy in fill(x):
            copy.wait()
        settle_slab(b, x, x, strip, fout.at[x], hout.at[x], at)
        for copy in store(x):
            copy.start()
        return carry

    lax.fori_loop(1, width - 1, settle, 0)
    for x in range(1, width - 1):
        for copy in store(x):
            copy.wait()


def settle_inner_call(place, fluid, heat, post, strip):
    width, _, depth, length = post.shape
    f32 = jnp.float32
    vmem = pl.BlockSpec(memory_space=pltpu.VMEM)
    hbm = pl.BlockSpec(memory_space=pl.ANY)
    return pl.pallas_call(
        settle_inner_kernel,
        in_specs=[pl.BlockSpec(memory_space=pltpu.SMEM), hbm, hbm, hbm, vmem],
        out_specs=[hbm, hbm],
        out_shape=[
            jax.ShapeDtypeStruct(fluid.shape, f32),
            jax.ShapeDtypeStruct(heat.shape, f32),
        ],
        scratch_shapes=[
            pltpu.VMEM((width, NP, depth, length), f32),
            pltpu.VMEM((width, NF, depth, length), f32),
            pltpu.VMEM((width, NH, depth, length), f32),
            pltpu.SemaphoreType.DMA((width,)),
            pltpu.SemaphoreType.DMA((2, width)),
            pltpu.SemaphoreType.DMA((2, width)),
        ],
        cost_estimate=cost(depth * width * length, 3),
        compiler_params=pltpu.CompilerParams(vmem_limit_bytes=28 * 2**20),
        name="settle_inner",
    )(place, in_hbm(fluid), in_hbm(heat), post, strip)


def settle_kernel(
    place,
    fluid,
    heat,
    post,
    west,
    east,
    strip_in,
    halo,
    kind,
    fluid_in,
    heat_in,
    fluid_out,
    heat_out,
    b,
    strip,
    fout,
    hout,
    load_sem,
    fill_sem,
    out_sem,
):
    width, depth, length = post.shape[0], post.shape[2], post.shape[3]
    tiles = length // TILE
    loads = [
        pltpu.make_async_copy(post.at[x], b.at[n], load_sem.at[n]) for x, n in ends_of(width)
    ]
    for n in range(2):
        x = n * (width - 1)
        loads.append(pltpu.make_async_copy(fluid.at[:, :, x], fout.at[n], fill_sem.at[0, n]))
        loads.append(pltpu.make_async_copy(heat.at[:, :, x], hout.at[n], fill_sem.at[1, n]))
    for copy in loads:
        copy.start()
    at = Lanes(depth, width, place)
    for p in range(NP):
        strip[p] = strip_in[p]
    ends_w, ends_e = west[NMOVE * tiles], east[NMOVE * tiles]
    close_strip(strip, halo[1], ends_w, ends_e, halo[0] > 0.5, at, width)
    close_faces(b, west, east, halo, kind[...].astype(jnp.float32), at)
    for copy in loads:
        copy.wait()

    def store(n):
        x = n * (width - 1)
        return (
            pltpu.make_async_copy(fout.at[n], fluid_out.at[:, :, x], out_sem.at[0, n]),
            pltpu.make_async_copy(hout.at[n], heat_out.at[:, :, x], out_sem.at[1, n]),
        )

    def settle(n, carry):
        settle_slab(b, n * (width - 1), 1 + 3 * n, strip, fout.at[n], hout.at[n], at)
        for copy in store(n):
            copy.start()
        return carry

    lax.fori_loop(0, 2, settle, 0)
    for n in range(2):
        for copy in store(n):
            copy.wait()


def settle_call(place, fluid, heat, post, west, east, strip, halo, kind, inner):
    width, _, depth, length = post.shape
    f32 = jnp.float32
    vmem = pl.BlockSpec(memory_space=pltpu.VMEM)
    hbm = pl.BlockSpec(memory_space=pl.ANY)
    return pl.pallas_call(
        settle_kernel,
        in_specs=[pl.BlockSpec(memory_space=pltpu.SMEM), hbm, hbm, hbm] + [vmem] * 5 + [hbm] * 2,
        out_specs=[hbm, hbm],
        out_shape=[
            jax.ShapeDtypeStruct(fluid.shape, f32),
            jax.ShapeDtypeStruct(heat.shape, f32),
        ],
        scratch_shapes=[
            pltpu.VMEM((6, NP, depth, length), f32),
            pltpu.VMEM((NP, depth, TILE), f32),
            pltpu.VMEM((2, NF, depth, length), f32),
            pltpu.VMEM((2, NH, depth, length), f32),
            pltpu.SemaphoreType.DMA((6,)),
            pltpu.SemaphoreType.DMA((2, 2)),
            pltpu.SemaphoreType.DMA((2, 2)),
        ],
        input_output_aliases={9: 0, 10: 1},
        cost_estimate=cost(depth * 2 * length, 3),
        compiler_params=pltpu.CompilerParams(vmem_limit_bytes=24 * 2**20),
        name="settle",
    )(place, in_hbm(fluid), in_hbm(heat), post, west, east, strip, halo, kind, *inner)


def ring(v, axis, shift):
    n = lax.axis_size(axis)
    return lax.ppermute(v, axis, [(i, (i + shift) % n) for i in range(n)])


def swap(v, axis, odd):
    n = lax.axis_size(axis)
    pairs = [(i, i + 1) for i in range(odd, n - 1, 2)]
    return lax.ppermute(v, axis, pairs + [(j, i) for i, j in pairs])


def per_device(fluid, heat, solid_mask, inflow_type):
    ew, ns = lax.axis_index("ew"), lax.axis_index("ns")
    ew_size, ns_size = lax.axis_size("ew"), lax.axis_size("ns")
    place = [ew == 0, ew == ew_size - 1, ns == 0, ns == ns_size - 1, ns % 2 == 1]
    place = jnp.stack(place).astype(jnp.int32)
    own = column_call(fluid, heat, solid_mask, inflow_type)
    even, odd = swap(own, "ns", 0), swap(own, "ns", 1)
    post, to_west, to_east = collide_call(fluid, heat, solid_mask)
    strip, to_west, to_east = strip_call(
        solid_mask.shape[1], place, own, even, odd, to_west, to_east
    )
    west, east = ring(to_east, "ew", 1), ring(to_west, "ew", -1)
    inner = advance_inner_call(place, post, strip)
    post, strip2, to_west, to_east, halo = advance_call(
        place, post, west, east, strip, inflow_type, inner
    )
    west, east = ring(to_east, "ew", 1), ring(to_west, "ew", -1)
    inner = settle_inner_call(place, fluid, heat, post, strip2)
    return settle_call(
        place, fluid, heat, post, west, east, strip2, halo, inflow_type, inner
    )


def solution(mesh):
    return jax.shard_map(
        per_device,
        mesh=mesh,
        in_specs=(
            P(None, None, "ew", "ns"),
            P(None, None, "ew", "ns"),
            P(None, "ew", "ns"),
            P(None, "ns"),
        ),
        out_specs=(P(None, None, "ew", "ns"), P(None, None, "ew", "ns")),
        check_vma=False,
    )
```

profile of v0, /device:TPU:1, one launch (start us, length us, event | category | flops | bytes accessed | tf_op | source)
XLA Modules:
  0.0 43.3 jit_solution(3987905002662631753)
XLA Ops:
  0.6 0.0 copy-start
  0.6 0.7 %copy-done = s32[32,256]{1,0:T(8,128)S(1)} copy-done((s32[32,256]{1,0:T(8,128)S(1)}, s32[32,256]{1,0:T(8,128)}, u32[]{:S(2)}) %copy-start) | copy-done | bytes 32792
  1.4 4.5 %columns.1.own = f32[7,32,128]{2,1,0:T(8,128)S(1)} custom-call(f32[19,256,256]{2,1,0:T(8,128)} %bitcast.8, f32[19,256,256]{2,1,0:T(8,128)} %bitcast.9, f32[7,256,256]{2,1,0:T(8,128)} %bitcast.12, f32[7,256,256]{2,1,0:T(8,128)} %bitcast.13, s32[256,256]{1,0:T(8,128)} %bitcast.16, s32[256,256]{1,0:T(8,128)} %bitcast.17, s32[32,256]{1,0:T(8,128)S(1)} %copy-done, ...), custom_call_target="tpu_custom_call" | custom-call | flops 39321600 | bytes 13631488 | tf_op jit(solution)/shard_map/columns/pallas_call | solution.py:189
  5.9 0.7 %collective-permute-start.1 = (f32[7,32,128]{2,1,0:T(8,128)S(1)}, f32[7,32,128]{2,1,0:T(8,128)S(1)}, u32[]{:S(2)}, u32[]{:S(2)}) collective-permute-start(f32[7,32,128]{2,1,0:T(8,128)S(1)} %columns.1.own), channel_id=1, source_target_pairs={{1,2},{2,1},{5,6},{6,5},{9,10},{10,9},{13,14},{14,13},{17,18},{18,... | collective-permute-start | bytes 344072 | tf_op jit(solution)/shard_map/ppermute | solution.py:749
  6.6 4.7 %collective-permute-start = (f32[7,32,128]{2,1,0:T(8,128)S(1)}, f32[7,32,128]{2,1,0:T(8,128)S(1)}, u32[]{:S(2)}, u32[]{:S(2)}) collective-permute-start(f32[7,32,128]{2,1,0:T(8,128)S(1)} %columns.1.own), channel_id=1, source_target_pairs={{0,1},{2,3},{1,0},{3,2},{4,5},{6,7},{5,4},{7,6},{8,9},{10,11},{9,8... | collective-permute-start | bytes 344072 | tf_op jit(solution)/shard_map/ppermute | solution.py:749
  11.3 0.1 stack.23
  11.4 5.9 %collide.1 = (f32[8,26,32,256]{3,2,1,0:T(8,128)S(1)}, f32[14,32,128]{2,1,0:T(8,128)S(1)}, f32[14,32,128]{2,1,0:T(8,128)S(1)}) custom-call(f32[19,256,256]{2,1,0:T(8,128)} %bitcast.10, f32[19,256,256]{2,1,0:T(8,128)} %bitcast.11, f32[7,256,256]{2,1,0:T(8,128)} %bitcast.14, f32[7,256,256]{2,1,0:T(8,128)} %bitcast.15, s32[256,256]{1,0:T(8,128)} %bitcast.18, ...), custom_call_target="tpu_custom_call" | custom-call | flops 39321600 | bytes 13631488 | tf_op jit(solution)/shard_map/collide/pallas_call | solution.py:226
  17.3 0.0 collective-permute-done.1.odd
  17.3 0.0 collective-permute-done.even
  17.3 1.5 %strips.1 = (f32[28,32,128]{2,1,0:T(8,128)S(1)}, f32[15,32,128]{2,1,0:T(8,128)S(1)}, f32[15,32,128]{2,1,0:T(8,128)S(1)}) custom-call(s32[5]{0:T(128)S(1)} %convert_element_type.3.place, f32[7,32,128]{2,1,0:T(8,128)S(1)} %columns.1.own, f32[7,32,128]{2,1,0:T(8,128)S(1)} %collective-permute-done.even, f32[7,32,128]{2,1,0:T(8,128)S(1)} %collective-permute-done.1.odd, ...), custom_call_target="tpu_custom_call" | custom-call | tf_op jit(solution)/shard_map/strips/pallas_call | solution.py:308
  18.8 2.4 %collective-permute-start.2 = (f32[15,32,128]{2,1,0:T(8,128)S(1)}, f32[15,32,128]{2,1,0:T(8,128)S(1)}, u32[]{:S(2)}, u32[]{:S(2)}) collective-permute-start(f32[15,32,128]{2,1,0:T(8,128)S(1)} %get-tuple-element.18), channel_id=1, source_target_pairs={{0,4},{4,8},{8,12},{12,16},{16,20},{20,24},{24,28},{28,0},{1,5},{5... | collective-permute-start | bytes 737288 | tf_op jit(solution)/shard_map/ppermute | solution.py:743
  21.2 0.0 collective-permute-start.3
  21.2 0.0 copy-start.1
  21.2 5.2 %advance_inner.1.next_in = f32[8,26,32,256]{3,2,1,0:T(8,128)S(1)} custom-call(s32[5]{0:T(128)S(1)} %convert_element_type.3.place, f32[8,26,32,256]{3,2,1,0:T(8,128)S(1)} %get-tuple-element.15.post, f32[28,32,128]{2,1,0:T(8,128)S(1)} %get-tuple-element.20.strip.strip_in), custom_call_target="tpu_custom_call" | custom-call | flops 39321600 | bytes 13631488 | tf_op jit(solution)/shard_map/advance_inner/pallas_call | solution.py:416
  26.4 0.0 collective-permute-done.2.west
  26.4 2.2 %collective-permute-done.3.east = f32[15,32,128]{2,1,0:T(8,128)S(1)} collective-permute-done((f32[15,32,128]{2,1,0:T(8,128)S(1)}, f32[15,32,128]{2,1,0:T(8,128)S(1)}, u32[]{:S(2)}, u32[]{:S(2)}) %collective-permute-start.3) | collective-permute-done | bytes 245792 | tf_op jit(solution)/shard_map/ppermute | solution.py:743
  28.6 0.0 copy-done.1
  28.6 2.8 %advance.1 = (f32[8,26,32,256]{3,2,1,0:T(8,128)S(1)}, f32[26,32,128]{2,1,0:T(8,128)S(1)}, f32[13,32,128]{2,1,0:T(8,128)S(1)}, f32[13,32,128]{2,1,0:T(8,128)S(1)}, f32[6,32,128]{2,1,0:T(8,128)S(1)}) custom-call(s32[5]{0:T(128)S(1)} %convert_element_type.3.place, f32[8,26,32,256]{3,2,1,0:T(8,128)S(1)} %get-tuple-element.15.post, ...), custom_call_target="tpu_custom_call", output_to_operand_aliasing={{0}: (6, {})} | custom-call | flops 14745600 | bytes 5111808 | tf_op jit(solution)/shard_map/advance/pallas_call | solution.py:526
  31.5 0.1 collective-permute-start.4
  31.5 0.5 %collective-permute-start.5 = (f32[13,32,128]{2,1,0:T(8,128)S(1)}, f32[13,32,128]{2,1,0:T(8,128)S(1)}, u32[]{:S(2)}, u32[]{:S(2)}) collective-permute-start(f32[13,32,128]{2,1,0:T(8,128)S(1)} %get-tuple-element.23), channel_id=1, source_target_pairs={{0,28},{4,0},{8,4},{12,8},{16,12},{20,16},{24,20},{28,24},{1,29},{... | collective-permute-start | bytes 638984 | tf_op jit(solution)/shard_map/ppermute | solution.py:743
  32.0 5.8 %settle_inner.1 = (f32[19,32,8,256]{3,2,1,0:T(8,128)}, f32[7,32,8,256]{3,2,1,0:T(8,128)}) custom-call(s32[5]{0:T(128)S(1)} %convert_element_type.3.place, f32[19,32,8,256]{3,2,1,0:T(8,128)} %fluid.3, f32[7,32,8,256]{3,2,1,0:T(8,128)} %heat.3, f32[8,26,32,256]{3,2,1,0:T(8,128)S(1)} %get-tuple-element.21.post, f32[26,32,128]{2,1,0:T(8,128)S(1)} %get-tuple-element.24.strip.strip_in), custom_call_target="tpu_custom_call" | custom-call | flops 58982400 | bytes 20447232 | tf_op jit(solution)/shard_map/settle_inner/pallas_call | solution.py:629
  37.9 0.0 collective-permute-done.4.west
  37.9 1.3 %collective-permute-done.5.east = f32[13,32,128]{2,1,0:T(8,128)S(1)} collective-permute-done((f32[13,32,128]{2,1,0:T(8,128)S(1)}, f32[13,32,128]{2,1,0:T(8,128)S(1)}, u32[]{:S(2)}, u32[]{:S(2)}) %collective-permute-start.5) | collective-permute-done | bytes 213024 | tf_op jit(solution)/shard_map/ppermute | solution.py:743
  39.1 4.1 %settle.1 = (f32[19,32,8,256]{3,2,1,0:T(8,128)}, f32[7,32,8,256]{3,2,1,0:T(8,128)}) custom-call(s32[5]{0:T(128)S(1)} %convert_element_type.3.place, f32[19,32,8,256]{3,2,1,0:T(8,128)} %fluid.3, f32[7,32,8,256]{3,2,1,0:T(8,128)} %heat.3, f32[8,26,32,256]{3,2,1,0:T(8,128)S(1)} %get-tuple-element.21.post, ...), custom_call_target="tpu_custom_call", output_to_operand_aliasing={{0}: (9, {}), {1}: (10, {})} | custom-call | flops 14745600 | bytes 5111808 | tf_op jit(solution)/shard_map/settle/pallas_call | solution.py:717
  (1 shorter events, 0.0 us)
Async XLA Ops:
  0.6 0.8 %copy-start = (s32[32,256]{1,0:T(8,128)S(1)}, s32[32,256]{1,0:T(8,128)}, u32[]{:S(2)}) copy-start(s32[32,256]{1,0:T(8,128)} %kind.3) | copy-start | bytes 98308
  5.9 11.4 %collective-permute-start.1 = (f32[7,32,128]{2,1,0:T(8,128)S(1)}, f32[7,32,128]{2,1,0:T(8,128)S(1)}, u32[]{:S(2)}, u32[]{:S(2)}) collective-permute-start(f32[7,32,128]{2,1,0:T(8,128)S(1)} %columns.1.own), channel_id=1, source_target_pairs={{1,2},{2,1},{5,6},{6,5},{9,10},{10,9},{13,14},{14,13},{17,18},{18,... | collective-permute-start | bytes 344072 | tf_op jit(solution)/shard_map/ppermute | solution.py:749
  6.6 10.7 %collective-permute-start = (f32[7,32,128]{2,1,0:T(8,128)S(1)}, f32[7,32,128]{2,1,0:T(8,128)S(1)}, u32[]{:S(2)}, u32[]{:S(2)}) collective-permute-start(f32[7,32,128]{2,1,0:T(8,128)S(1)} %columns.1.own), channel_id=1, source_target_pairs={{0,1},{2,3},{1,0},{3,2},{4,5},{6,7},{5,4},{7,6},{8,9},{10,11},{9,8... | collective-permute-start | bytes 344072 | tf_op jit(solution)/shard_map/ppermute | solution.py:749
  18.8 7.6 %collective-permute-start.2 = (f32[15,32,128]{2,1,0:T(8,128)S(1)}, f32[15,32,128]{2,1,0:T(8,128)S(1)}, u32[]{:S(2)}, u32[]{:S(2)}) collective-permute-start(f32[15,32,128]{2,1,0:T(8,128)S(1)} %get-tuple-element.18), channel_id=1, source_target_pairs={{0,4},{4,8},{8,12},{12,16},{16,20},{20,24},{24,28},{28,0},{1,5},{5... | collective-permute-start | bytes 737288 | tf_op jit(solution)/shard_map/ppermute | solution.py:743
  21.2 7.4 %collective-permute-start.3 = (f32[15,32,128]{2,1,0:T(8,128)S(1)}, f32[15,32,128]{2,1,0:T(8,128)S(1)}, u32[]{:S(2)}, u32[]{:S(2)}) collective-permute-start(f32[15,32,128]{2,1,0:T(8,128)S(1)} %get-tuple-element.19), channel_id=1, source_target_pairs={{0,28},{4,0},{8,4},{12,8},{16,12},{20,16},{24,20},{28,24},{1,29},{... | collective-permute-start | bytes 737288 | tf_op jit(solution)/shard_map/ppermute | solution.py:743
  21.2 7.4 %copy-start.1 = (s32[32,256]{1,0:T(8,128)S(1)}, s32[32,256]{1,0:T(8,128)}, u32[]{:S(2)}) copy-start(s32[32,256]{1,0:T(8,128)} %kind.3) | copy-start | bytes 98308
  31.5 6.4 %collective-permute-start.4 = (f32[13,32,128]{2,1,0:T(8,128)S(1)}, f32[13,32,128]{2,1,0:T(8,128)S(1)}, u32[]{:S(2)}, u32[]{:S(2)}) collective-permute-start(f32[13,32,128]{2,1,0:T(8,128)S(1)} %get-tuple-element.22), channel_id=1, source_target_pairs={{0,4},{4,8},{8,12},{12,16},{16,20},{20,24},{24,28},{28,0},{1,5},{5... | collective-permute-start | bytes 638984 | tf_op jit(solution)/shard_map/ppermute | solution.py:743
  31.5 7.6 %collective-permute-start.5 = (f32[13,32,128]{2,1,0:T(8,128)S(1)}, f32[13,32,128]{2,1,0:T(8,128)S(1)}, u32[]{:S(2)}, u32[]{:S(2)}) collective-permute-start(f32[13,32,128]{2,1,0:T(8,128)S(1)} %get-tuple-element.23), channel_id=1, source_target_pairs={{0,28},{4,0},{8,4},{12,8},{16,12},{20,16},{24,20},{28,24},{1,29},{... | collective-permute-start | bytes 638984 | tf_op jit(solution)/shard_map/ppermute | solution.py:743
where the time goes:
time: 43.8 us; the launch traced here: 43.3 us
  Pallas kernels  29.8 us (68%)
  starting transfers between devices  8.33 us (19%)
  waiting for transfers between devices  3.49 us (8%)
  local copies, waits for them, and re-layouts  0.86 us (2%)
  between operations  0.74 us (2%)
    pallas_call x1, Pallas kernels, collide_call(): pl.pallas_call(functools.partial(collide_kernel, tiles), grid=(depth // r...  5.88 us
    pallas_call x1, Pallas kernels, settle_inner_call(): pl.pallas_call(settle_inner_kernel, in_specs=[pl.BlockSpec(memory_space=p...  5.81 us
    ppermute x2, starting transfers between devices, swap(): return lax.ppermute(v, axis, pairs + [(j, i) for i, j in pairs])  5.38 us
    pallas_call x1, Pallas kernels, advance_inner_call(): pl.pallas_call(advance_inner_kernel, in_specs=[pl.BlockSpec(memory_space=...  5.2 us
    pallas_call x1, Pallas kernels, column_call(): pl.pallas_call(functools.partial(column_kernel, width), grid=(depth // ro...  4.51 us
    pallas_call x1, Pallas kernels, settle_call(): pl.pallas_call(settle_kernel, in_specs=[pl.BlockSpec(memory_space=pltpu.S...  4.12 us
    ppermute x4, waiting for transfers between devices, ring(): return lax.ppermute(v, axis, [(i, (i + shift) % n) for i in range(n)])  3.48 us
    ppermute x4, starting transfers between devices, ring(): return lax.ppermute(v, axis, [(i, (i + shift) % n) for i in range(n)])  2.94 us
  transfers between devices with their start and end apart: 6, of which 2 were waited for; matrix products, arithmetic and copies ran while one was open for 0% of the time, Pallas kernels for 39%

commit v1 on v0

v1 whole, which is shorter than its diff:
```python
import functools
import math

import jax
import jax.numpy as jnp
from jax import lax
from jax.experimental import pallas as pl
from jax.experimental.pallas import tpu as pltpu
from jax.sharding import PartitionSpec as P

FLUID_DIRS = [
    (0, 0, 0),
    (1, 0, 0),
    (-1, 0, 0),
    (0, 1, 0),
    (0, -1, 0),
    (0, 0, 1),
    (0, 0, -1),
    (1, 1, 0),
    (-1, -1, 0),
    (1, -1, 0),
    (-1, 1, 0),
    (1, 0, 1),
    (-1, 0, -1),
    (1, 0, -1),
    (-1, 0, 1),
    (0, 1, 1),
    (0, -1, -1),
    (0, 1, -1),
    (0, -1, 1),
]
DIRS = FLUID_DIRS + FLUID_DIRS[:7]
NF, NH = 19, 7
NP = NF + NH
OPP = [
    (FLUID_DIRS.index((-c[0], -c[1], -c[2])) + (0 if i < NF else NF)) for i, c in enumerate(DIRS)
]
WEIGHTS = (
    [1.0 / 3.0] + [1.0 / 18.0] * 6 + [1.0 / 36.0] * 12 + [0.25] + [0.125] * 6
)
PLUS = [i for i, c in enumerate(DIRS) if c[0] == 1]
MINUS = [i for i, c in enumerate(DIRS) if c[0] == -1]
TAU = 0.6
TAU_HEAT = 0.8
COUPLING = 0.02
INFLOW_SPEED = 0.08
COOLING = 0.2
MARK = float("nan")
MASK, KIND = NP, NP + 1
SLOTS = NP + 2
NMOVE = len(PLUS)
NFACE = NMOVE + 1
TILE = 128
GROUP = 4
GROUPS = SLOTS // GROUP
PITCH = TILE // GROUP


def collided(f, solid):
    pairs = {k: (f[k] + f[k + 1], f[k] - f[k + 1]) for k in range(1, NF, 2)}
    s = {k: v[0] for k, v in pairs.items()}
    d = {k: v[1] for k, v in pairs.items()}
    rho = (f[0] + (s[1] + s[3])) + ((s[5] + s[7]) + (s[9] + s[11])) + ((s[13] + s[15]) + s[17])
    mx = (d[1] + d[7]) + (d[9] + (d[11] + d[13]))
    my = (d[3] + d[7]) + ((d[15] - d[9]) + d[17])
    mz = (d[5] + d[11]) + ((d[15] - d[13]) - d[17])
    g = f[NF:]
    hp = [(g[k] + g[k + 1]) for k in (1, 3, 5)]
    warm = (g[0] + hp[0]) + (hp[1] + hp[2])
    inv = 1.0 / rho
    ux, uy, uz = mx * inv, my * inv, mz * inv
    lifted = uz + TAU * COUPLING * (warm - 1.0)
    root = math.sqrt(4.5)
    ax, ay, az = ux * root, uy * root, lifted * root
    base = 1.0 - (ax * ax + ay * ay + az * az) * (1.0 / 3.0)
    keep = 1.0 - 1.0 / TAU
    r = jnp.where(solid, MARK, rho * (1.0 / TAU))
    r18, r36 = r * (1.0 / 18.0), r * (1.0 / 36.0)
    o18, o36 = r18 * (3.0 / root), r36 * (3.0 / root)
    out = [None] * NP
    out[0] = keep * f[0] + (r * (1.0 / 3.0)) * base
    along = {
        1: ax,
        3: ay,
        5: az,
        7: ax + ay,
        9: ax - ay,
        11: ax + az,
        13: ax - az,
        15: ay + az,
        17: ay - az,
    }
    for k, e in along.items():
        w, o = (r18, o18) if k < 7 else (r36, o36)
        even = w * (base + e * e)
        odd = o * e
        out[k] = keep * f[k] + (even + odd)
        out[k + 1] = keep * f[k + 1] + (even - odd)
    hkeep = 1.0 - 1.0 / TAU_HEAT
    t8 = jnp.where(solid, MARK, warm * (0.125 / TAU_HEAT))
    out[NF] = hkeep * g[0] + (t8 + t8)
    t2 = t8 * 4.0
    for k, u in ((1, ux), (3, uy), (5, uz)):
        odd = t2 * u
        out[NF + k] = hkeep * g[k] + (t8 + odd)
        out[NF + k + 1] = hkeep * g[k + 1] + (t8 - odd)
    return out


def ghost(i, kind):
    u = (INFLOW_SPEED * 0.5) * kind
    cx = DIRS[i][0]
    if i < NF:
        return WEIGHTS[i] * (1.0 + 3.0 * cx * u + (4.5 * cx * cx - 1.5) * (u * u))
    return WEIGHTS[i] * (1.0 - COOLING * kind) * (1.0 + 4.0 * cx * u)


def marked(v):
    return v != v


def clean(v):
    return jnp.where(marked(v), 0.0, v)


def collide_slab(x, before, solid, post):
    depth, length = post.shape[2], post.shape[3]
    for z in range(0, depth, 8):
        for t in range(length // TILE):
            part, span = pl.ds(z, 8), pl.ds(t * TILE, TILE)
            f = [before[x, i, part, span] for i in range(NP)]
            for i, v in enumerate(collided(f, solid[x, part, span] > 0)):
                post[x, i, part, span] = v


def collide_kernel(before, solid, post, west, east):
    width, length = post.shape[0], post.shape[3]
    tiles = length // TILE

    def collide(x, carry):
        collide_slab(x, before, solid, post)
        return carry

    lax.fori_loop(0, width, collide, 0)
    for face, near, moving in ((west, 0, MINUS), (east, width - 1, PLUS)):
        for t in range(tiles):
            span = pl.ds(t * TILE, TILE)
            for n, i in enumerate(moving):
                face[n * tiles + t] = clean(post[near, i, :, span])
            face[NMOVE * tiles + t] = jnp.where(solid[near, :, span] > 0, 1.0, 0.0)


def collide_call(before, solid):
    width, _, depth, length = before.shape
    face = jax.ShapeDtypeStruct((NFACE * (length // TILE), depth, TILE), jnp.float32)
    vmem = pl.BlockSpec(memory_space=pltpu.VMEM)
    return pl.pallas_call(
        collide_kernel,
        in_specs=[vmem, vmem],
        out_specs=[vmem, vmem, vmem],
        out_shape=[jax.ShapeDtypeStruct(before.shape, jnp.float32), face, face],
        cost_estimate=cost(depth * width * length, 2),
        compiler_params=pltpu.CompilerParams(vmem_limit_bytes=16 * 2**20),
        name="collide",
    )(before, solid)


def column_kernel(place, fluid, heat, mask, kind, packed, before, solid, kinds, total, sem, kind_sem):
    width, depth, length = solid.shape
    shape = (depth, TILE)
    lanes = lax.broadcasted_iota(jnp.int32, shape, 1)
    start, stop = lanes < 2, lanes >= TILE - 2
    first, last = pl.ds(0, TILE), pl.ds(length - TILE, TILE)

    def fetch(x):
        return (
            pltpu.make_async_copy(mask.at[:, x], solid.at[x], sem.at[x, 0]),
            pltpu.make_async_copy(fluid.at[:, :, x], before.at[x, pl.ds(0, NF)], sem.at[x, 1]),
            pltpu.make_async_copy(heat.at[:, :, x], before.at[x, pl.ds(NF, NH)], sem.at[x, 2]),
        )

    for x in range(width):
        for copy in fetch(x):
            copy.start()
    fetch_kind = pltpu.make_async_copy(kind, kinds, kind_sem)
    fetch_kind.start()
    for p in range(SLOTS):
        total[p] = jnp.zeros(shape, jnp.float32)
    fetch_kind.wait()
    k = [kinds[:, first].astype(jnp.float32), kinds[:, last].astype(jnp.float32)]
    kind_ends = jnp.where(stop, k[1], jnp.where(start, k[0], 0.0))

    def gather(x, carry):
        for copy in fetch(x):
            copy.wait()
        shift = x * 4 + 2
        for i in range(NP):
            ends = jnp.where(stop, before[x, i, :, last], before[x, i, :, first])
            ends = jnp.where(start | stop, ends, 0.0)
            total[i] = total[i] + pltpu.roll(ends, shift, 1)
        ends = jnp.where(stop, solid[x, :, last], solid[x, :, first]).astype(jnp.float32)
        ends = jnp.where(start | stop, ends, 0.0)
        total[MASK] = total[MASK] + pltpu.roll(ends, shift, 1)
        total[KIND] = total[KIND] + pltpu.roll(kind_ends, shift, 1)
        return carry

    lax.fori_loop(0, width, gather, 0)
    for z in range(0, depth, 8):
        part = pl.ds(z, 8)
        f = [total[i, part] for i in range(NP)]
        filled = total[MASK, part] > 0.5
        idle = filled | (lanes[z : z + 8] >= 4 * width)
        out = [jnp.where(idle, 0.0, v) for v in collided(f, filled)]
        out += [total[MASK, part], total[KIND, part]]
        for group in range(GROUPS):
            v = out[group * GROUP]
            for k in range(1, GROUP):
                v = v + pltpu.roll(out[group * GROUP + k], k * PITCH, 1)
            packed[group, part] = v


def column_call(place, fluid, heat, mask, kind):
    depth, width, length = mask.shape
    f32 = jnp.float32
    vmem = pl.BlockSpec(memory_space=pltpu.VMEM)
    hbm = pl.BlockSpec(memory_space=pl.ANY)
    return pl.pallas_call(
        column_kernel,
        in_specs=[pl.BlockSpec(memory_space=pltpu.SMEM)] + [hbm] * 4,
        out_specs=[vmem] * 3,
        out_shape=[
            jax.ShapeDtypeStruct((GROUPS, depth, TILE), f32),
            jax.ShapeDtypeStruct((width, NP, depth, length), f32),
            jax.ShapeDtypeStruct((width, depth, length), jnp.int32),
        ],
        scratch_shapes=[
            pltpu.VMEM((depth, length), jnp.int32),
            pltpu.VMEM((SLOTS, depth, TILE), f32),
            pltpu.SemaphoreType.DMA((width, 3)),
            pltpu.SemaphoreType.DMA,
        ],
        cost_estimate=cost(depth * width * length, 2),
        compiler_params=pltpu.CompilerParams(vmem_limit_bytes=16 * 2**20),
        name="columns",
    )(place, *[in_hbm(v) for v in (fluid, heat, mask, kind)])


def in_hbm(v):
    return pltpu.with_memory_space_constraint(v, pltpu.HBM)


def cost(cells, passes):
    return pl.CostEstimate(
        flops=300 * cells * passes, bytes_accessed=4 * NP * cells * passes, transcendentals=0
    )


class Lanes:
    def __init__(self, depth, place):
        shape = (depth, TILE)
        lane = lax.broadcasted_iota(jnp.int32, shape, 1)
        level = lax.broadcasted_iota(jnp.int32, shape, 0)
        self.side, self.slot, self.j = lane // 64, (lane % 64) // 4, lane % 4
        self.ground, self.top = level == 0, level == depth - 1
        self.first, self.last = lane == 0, lane == TILE - 1
        self.west, self.east = place[0] == 1, place[1] == 1
        low = (place[2] == 1) & (self.side == 0) & (self.j < 2)
        high = (place[3] == 1) & (self.side == 1) & (self.j >= 2)
        self.beyond_y = low | high


def strip_kernel(width, place, own, even, odd, after, strip, to_west, to_east):
    depth = own.shape[1]
    at = Lanes(depth, place)
    flip = place[4] == 1
    slots_w = [None] * NFACE
    slots_e = [None] * NFACE
    near_j = at.j < 2
    for group in range(GROUPS):
        o = own[group]
        above = jnp.where(flip, odd[group], even[group])
        below = jnp.where(flip, even[group], odd[group])
        low, high = jnp.where(near_j, below, o), jnp.where(near_j, o, above)
        for k in range(GROUP):
            p = group * GROUP + k
            v = jnp.where(
                at.side == 0,
                pltpu.roll(low, (16 - k * PITCH) % TILE, 1),
                pltpu.roll(high, (80 - k * PITCH) % TILE, 1),
            )
            strip[p] = v
            if p in MINUS or p == MASK:
                n = NMOVE if p == MASK else MINUS.index(p)
                slots_w[n] = pltpu.roll(v, (4 * n - 16) % TILE, 1)
            if p in PLUS or p == MASK:
                n = NMOVE if p == MASK else PLUS.index(p)
                slots_e[n] = pltpu.roll(v, (4 * n - 12 - 4 * width) % TILE, 1)
    for out, slots in ((to_west, slots_w), (to_east, slots_e)):
        total = jnp.zeros_like(slots[0])
        for n, v in enumerate(slots):
            total = jnp.where(at.slot == n, v, total)
        out[...] = total
    solid = strip[MASK] > 0.5
    for i in range(NP):
        strip[i] = jnp.where(at.beyond_y, WEIGHTS[i], jnp.where(solid, MARK, strip[i]))


def strip_call(width, place, own, even, odd, after):
    _, depth, _ = own.shape
    f32 = jnp.float32
    vmem = pl.BlockSpec(memory_space=pltpu.VMEM)
    return pl.pallas_call(
        functools.partial(strip_kernel, width),
        in_specs=[pl.BlockSpec(memory_space=pltpu.SMEM)]
        + [vmem] * 3
        + [pl.BlockSpec(memory_space=pl.ANY)],
        out_specs=[vmem, vmem, vmem],
        out_shape=[
            jax.ShapeDtypeStruct((SLOTS, depth, TILE), f32),
            jax.ShapeDtypeStruct((depth, TILE), f32),
            jax.ShapeDtypeStruct((depth, TILE), f32),
        ],
        compiler_params=pltpu.CompilerParams(vmem_limit_bytes=8 * 2**20),
        name="strips",
    )(place, own, even, odd, after)


def raised(v, i, at):
    depth = v.shape[0]
    cz = DIRS[i][2]
    if cz == 1:
        return jnp.where(at.ground, MARK, pltpu.roll(v, 1, 0))
    if cz == -1:
        return jnp.where(at.top, WEIGHTS[i], pltpu.roll(v, depth - 1, 0))
    return v


def pieces(ref, index, i, tiles):
    return [ref[index, i, :, pl.ds(t * TILE, TILE)] for t in range(tiles)]


def turned(v, shift):
    shift = shift % TILE if isinstance(shift, int) else lax.rem(shift + 4 * TILE, TILE)
    return pltpu.roll(v, shift, 1)


def pulled(cells, cols, x, i, at):
    cx, cy, _ = DIRS[i]
    source = cells(x - cx, i)
    if cy:
        moved = [turned(v, cy) for v in source]
        lane = (x - cx + 4) * 4
        if cy == 1:
            before = [turned(cols[i], -1 - lane)] + moved[:-1]
            source = [jnp.where(at.first, p, v) for p, v in zip(before, moved)]
        else:
            after = moved[1:] + [turned(cols[i], TILE - 1 - (64 + lane + 2))]
            source = [jnp.where(at.last, n, v) for n, v in zip(after, moved)]
    return [raised(v, i, at) for v in source]


def close_strip(strip, kinds, from_west, from_east, solid, at, width):
    kind = jnp.where(at.beyond_y, 0.0, kinds)
    for face, edge, slot, moving in (
        (from_west, at.west, 3, PLUS),
        (from_east, at.east, 4 + width, MINUS),
    ):
        here = at.slot == slot
        for n, i in enumerate(moving):
            v = pltpu.roll(face, (4 * slot - 4 * n) % TILE, 1)
            v = jnp.where(solid, MARK, v)
            v = jnp.where(at.beyond_y, WEIGHTS[i], v)
            v = jnp.where(edge, ghost(i, kind) if slot == 3 else WEIGHTS[i], v)
            strip[i] = jnp.where(here, v, strip[i])


def layers(ref, tiles, halo=None):
    def cells(x, i):
        if halo is not None and isinstance(x, int) and not 0 <= x < ref.shape[0]:
            return pieces(halo, 0 if x < 0 else 1, i, tiles)
        return pieces(ref, x, i, tiles)

    return cells


def advance_slab(cells, x, strip, fresh, out, at):
    depth, length = fresh.shape[1], fresh.shape[2]
    tiles = length // TILE
    for i in range(NP):
        vs = pulled(cells, strip, x, i, at)
        for t, (v, back) in enumerate(zip(vs, cells(x, OPP[i]))):
            fresh[i, :, pl.ds(t * TILE, TILE)] = jnp.where(marked(v), back, v)
    own = cells(x, 0)
    for z in range(0, depth, 8):
        for t in range(tiles):
            part, span = pl.ds(z, 8), pl.ds(t * TILE, TILE)
            f = [fresh[i, part, span] for i in range(NP)]
            solid = marked(own[t][z : z + 8])
            for i, v in enumerate(collided(f, solid)):
                out[x, i, part, span] = v


def advance_inner_kernel(low, high, place, post, strip, *refs):
    out, fresh = refs[-2:]
    depth, length = post.shape[2], post.shape[3]
    at = Lanes(depth, place)
    cells = layers(post, length // TILE)

    def advance(x, carry):
        advance_slab(cells, x, strip, fresh, out, at)
        return carry

    lax.fori_loop(low, high, advance, 0)


def advance_inner_call(place, post, strip, low, high, *others):
    width, _, depth, length = post.shape
    f32 = jnp.float32
    vmem = pl.BlockSpec(memory_space=pltpu.VMEM)
    return pl.pallas_call(
        functools.partial(advance_inner_kernel, low, high),
        in_specs=[pl.BlockSpec(memory_space=pltpu.SMEM)] + [vmem] * (2 + len(others)),
        out_specs=vmem,
        out_shape=jax.ShapeDtypeStruct((width, NP, depth, length), f32),
        scratch_shapes=[pltpu.VMEM((NP, depth, length), f32)],
        input_output_aliases={3: 0} if others else {},
        cost_estimate=cost(depth * (high - low) * length, 4),
        compiler_params=pltpu.CompilerParams(vmem_limit_bytes=16 * 2**20),
        name="advance_inner",
    )(place, post, strip, *others)


def advance_kernel(
    place,
    post,
    west,
    east,
    strip_in,
    strip_w,
    strip_e,
    kind,
    next_in,
    next_out,
    strip2,
    to_west,
    to_east,
    halo,
    a,
    strip,
    fresh,
):
    width, depth, length = post.shape[0], post.shape[2], post.shape[3]
    tiles = length // TILE
    at = Lanes(depth, place)
    for p in range(SLOTS):
        strip[p] = strip_in[p]
    ends_w, ends_e = strip_w[...], strip_e[...]
    ends = jnp.where(
        at.slot == 3,
        pltpu.roll(ends_w, (12 - 4 * NMOVE) % TILE, 1),
        pltpu.roll(ends_e, (16 + 4 * width - 4 * NMOVE) % TILE, 1),
    )
    kind_end = pltpu.roll(strip[KIND], TILE - 4, 1)
    close_strip(strip, kind_end, ends_w, ends_e, ends > 0.5, at, width)
    halo[0], halo[1] = ends, kind_end
    for n, face in ((2, west), (2 + tiles, east)):
        for t in range(tiles):
            halo[n + t] = face[NMOVE * tiles + t]
    kinds = kind[...].astype(jnp.float32)
    close_faces(a, west, east, halo, kinds, at)

    for i in range(NP):
        cx, cy, _ = DIRS[i]
        v = strip[i]
        if cx or cy:
            v = pltpu.roll(v, (4 * cx + cy) % TILE, 1)
        v = raised(v, i, at)
        fresh[i, :, pl.ds(0, TILE)] = jnp.where(marked(v), strip[OPP[i]], v)
    for z in range(0, depth, 8):
        part = pl.ds(z, 8)
        f = [fresh[i, part, pl.ds(0, TILE)] for i in range(NP)]
        outside = at.beyond_y[z : z + 8]
        for i, v in enumerate(collided(f, marked(strip[0, part]))):
            strip2[i, part] = jnp.where(outside, WEIGHTS[i], v)

    cells = layers(post, tiles, a)
    for x in (0, width - 1):
        advance_slab(cells, x, strip, fresh, next_out, at)
    for out, near, moving in ((to_west, 0, MINUS), (to_east, width - 1, PLUS)):
        slots = None
        for n, i in enumerate(moving):
            for t in range(tiles):
                out[n * tiles + t] = clean(next_out[near, i, :, pl.ds(t * TILE, TILE)])
            v = pltpu.roll(clean(strip2[i]), (4 * n - 4 * (near + 4)) % TILE, 1)
            slots = v if slots is None else jnp.where(at.slot == n, v, slots)
        out[NMOVE * tiles] = slots


def advance_call(place, post, west, east, strip, strip_w, strip_e, kind, inner):
    width, _, depth, length = post.shape
    tiles = length // TILE
    f32 = jnp.float32
    vmem = pl.BlockSpec(memory_space=pltpu.VMEM)
    sends = NMOVE * tiles + 1
    return pl.pallas_call(
        advance_kernel,
        in_specs=[pl.BlockSpec(memory_space=pltpu.SMEM)] + [vmem] * 8,
        out_specs=[vmem] * 5,
        out_shape=[
            jax.ShapeDtypeStruct((width, NP, depth, length), f32),
            jax.ShapeDtypeStruct((NP, depth, TILE), f32),
            jax.ShapeDtypeStruct((sends, depth, TILE), f32),
            jax.ShapeDtypeStruct((sends, depth, TILE), f32),
            jax.ShapeDtypeStruct((2 + 2 * tiles, depth, TILE), f32),
        ],
        scratch_shapes=[
            pltpu.VMEM((2, NP, depth, length), f32),
            pltpu.VMEM((SLOTS, depth, TILE), f32),
            pltpu.VMEM((NP, depth, length), f32),
        ],
        input_output_aliases={8: 0},
        cost_estimate=cost(depth * 2 * length, 3),
        compiler_params=pltpu.CompilerParams(vmem_limit_bytes=24 * 2**20),
        name="advance",
    )(place, post, west, east, strip, strip_w, strip_e, kind, inner)


def close_faces(a, west, east, halo, kinds, at):
    tiles = a.shape[3] // TILE
    for face, edge, near, moving in (
        (west, at.west, 0, PLUS),
        (east, at.east, 1, MINUS),
    ):
        for t in range(tiles):
            solid = halo[2 + t if near == 0 else 2 + tiles + t] > 0.5
            span = slice(t * TILE, (t + 1) * TILE)
            for n, i in enumerate(moving):
                v = jnp.where(solid, MARK, face[n * tiles + t])
                outer = ghost(i, kinds[:, span]) if near == 0 else WEIGHTS[i]
                a[near, i, :, span] = jnp.where(edge, outer, v)


def settle_slab(cells, x, strip, before, out, at):
    solids = [marked(v) for v in cells(x, 0)]
    for i in range(NP):
        vs = pulled(cells, strip, x, i, at)
        for t, (v, back) in enumerate(zip(vs, cells(x, OPP[i]))):
            span = pl.ds(t * TILE, TILE)
            v = jnp.where(marked(v), back, v)
            out[i, :, span] = jnp.where(solids[t], before[x, i, :, span], v)


def stores(buffer, fluid_out, heat_out, x, sem):
    return (
        pltpu.make_async_copy(buffer.at[pl.ds(0, NF)], fluid_out.at[:, :, x], sem.at[0]),
        pltpu.make_async_copy(buffer.at[pl.ds(NF, NH)], heat_out.at[:, :, x], sem.at[1]),
    )


def settle_inner_kernel(place, before, post, strip, fluid_out, heat_out, buffer, sem):
    width, depth, length = post.shape[0], post.shape[2], post.shape[3]
    at = Lanes(depth, place)
    cells = layers(post, length // TILE)

    def settle(x, carry):
        settle_slab(cells, x, strip, before, buffer.at[x], at)
        for copy in stores(buffer.at[x], fluid_out, heat_out, x, sem.at[x]):
            copy.start()
        return carry

    lax.fori_loop(1, width - 1, settle, 0)
    for x in range(1, width - 1):
        for copy in stores(buffer.at[x], fluid_out, heat_out, x, sem.at[x]):
            copy.wait()


def settle_inner_call(place, before, post, strip, outs):
    width, _, depth, length = post.shape
    vmem = pl.BlockSpec(memory_space=pltpu.VMEM)
    hbm = pl.BlockSpec(memory_space=pl.ANY)
    return pl.pallas_call(
        settle_inner_kernel,
        in_specs=[pl.BlockSpec(memory_space=pltpu.SMEM)] + [vmem] * 3,
        out_specs=[hbm, hbm],
        out_shape=[jax.ShapeDtypeStruct(v.shape, v.dtype) for v in outs],
        scratch_shapes=[
            pltpu.VMEM((width, NP, depth, length), jnp.float32),
            pltpu.SemaphoreType.DMA((width, 2)),
        ],
        cost_estimate=cost(depth * width * length, 3),
        compiler_params=pltpu.CompilerParams(vmem_limit_bytes=24 * 2**20),
        name="settle_inner",
    )(place, before, post, strip)


def settle_kernel(
    place,
    before,
    post,
    west,
    east,
    strip_in,
    halo,
    kind,
    fluid_in,
    heat_in,
    fluid_out,
    heat_out,
    b,
    strip,
    buffer,
    sem,
):
    width, depth, length = post.shape[0], post.shape[2], post.shape[3]
    tiles = length // TILE
    at = Lanes(depth, place)
    for p in range(NP):
        strip[p] = strip_in[p]
    ends_w, ends_e = west[NMOVE * tiles], east[NMOVE * tiles]
    close_strip(strip, halo[1], ends_w, ends_e, halo[0] > 0.5, at, width)
    close_faces(b, west, east, halo, kind[...].astype(jnp.float32), at)
    cells = layers(post, tiles, b)
    ends = ((0, 0), (1, width - 1))
    for n, x in ends:
        settle_slab(cells, x, strip, before, buffer.at[n], at)
        for copy in stores(buffer.at[n], fluid_out, heat_out, x, sem.at[n]):
            copy.start()
    for n, x in ends:
        for copy in stores(buffer.at[n], fluid_out, heat_out, x, sem.at[n]):
            copy.wait()


def settle_call(place, before, post, west, east, strip, halo, kind, inner):
    _, _, depth, length = post.shape
    f32 = jnp.float32
    vmem = pl.BlockSpec(memory_space=pltpu.VMEM)
    hbm = pl.BlockSpec(memory_space=pl.ANY)
    return pl.pallas_call(
        settle_kernel,
        in_specs=[pl.BlockSpec(memory_space=pltpu.SMEM)] + [vmem] * 7 + [hbm] * 2,
        out_specs=[hbm, hbm],
        out_shape=[jax.ShapeDtypeStruct(v.shape, v.dtype) for v in inner],
        scratch_shapes=[
            pltpu.VMEM((2, NP, depth, length), f32),
            pltpu.VMEM((NP, depth, TILE), f32),
            pltpu.VMEM((2, NP, depth, length), f32),
            pltpu.SemaphoreType.DMA((2, 2)),
        ],
        input_output_aliases={8: 0, 9: 1},
        cost_estimate=cost(depth * 2 * length, 3),
        compiler_params=pltpu.CompilerParams(vmem_limit_bytes=24 * 2**20),
        name="settle",
    )(place, before, post, west, east, strip, halo, kind, *inner)


def ring(v, axis, shift):
    n = lax.axis_size(axis)
    return lax.ppermute(v, axis, [(i, (i + shift) % n) for i in range(n)])


def swap(v, axis, odd):
    n = lax.axis_size(axis)
    pairs = [(i, i + 1) for i in range(odd, n - 1, 2)]
    return lax.ppermute(v, axis, pairs + [(j, i) for i, j in pairs])


def per_device(fluid, heat, solid_mask, inflow_type):
    ew, ns = lax.axis_index("ew"), lax.axis_index("ns")
    ew_size, ns_size = lax.axis_size("ew"), lax.axis_size("ns")
    place = [ew == 0, ew == ew_size - 1, ns == 0, ns == ns_size - 1, ns % 2 == 1]
    place = jnp.stack(place).astype(jnp.int32)
    width = solid_mask.shape[1]
    own, before, solid = column_call(place, fluid, heat, solid_mask, inflow_type)
    even = swap(own, "ns", 0)
    odd = swap(own, "ns", 1)
    post, to_west, to_east = collide_call(before, solid)
    west, east = ring(to_east, "ew", 1), ring(to_west, "ew", -1)
    strip, to_west, to_east = strip_call(width, place, own, even, odd, to_west)
    strip_w, strip_e = ring(to_east, "ew", 1), ring(to_west, "ew", -1)
    middle = width // 2
    done = advance_inner_call(place, post, strip, 1, middle)
    done, strip2, to_west, to_east, halo = advance_call(
        place, post, west, east, strip, strip_w, strip_e, inflow_type, done
    )
    west, east = ring(to_east, "ew", 1), ring(to_west, "ew", -1)
    post = advance_inner_call(place, post, strip, middle, width - 1, done)
    inner = settle_inner_call(place, before, post, strip2, (fluid, heat))
    return settle_call(place, before, post, west, east, strip2, halo, inflow_type, inner)


def solution(mesh):
    return jax.shard_map(
        per_device,
        mesh=mesh,
        in_specs=(
            P(None, None, "ew", "ns"),
            P(None, None, "ew", "ns"),
            P(None, "ew", "ns"),
            P(None, "ns"),
        ),
        out_specs=(P(None, None, "ew", "ns"), P(None, None, "ew", "ns")),
        check_vma=False,
    )
```

time: 43.8 us -> 39.1 us (0.89)
  Pallas kernels: 29.8 us -> 20.1 us
  starting transfers between devices: 8.33 us -> 11.3 us
  waiting for transfers between devices: 3.49 us -> 6.34 us
  local copies, waits for them, and re-layouts: 0.86 us -> 0.11 us
    pallas_call x3 -> x4, Pallas kernels: 15.6 us -> 11.7 us  [the longest x1 5.71 us: column_call(): pl.pallas_call(column_kernel, in_specs=[pl.BlockSpec(memory_space=pltpu.S...]
    ppermute x4 -> x6, starting transfers between devices: 2.94 us -> 6.71 us  [ring(): return lax.ppermute(v, axis, [(i, (i + shift) % n) for i in range(n)])]
    pallas_call x1, Pallas kernels: 5.81 us -> 3.22 us  [settle_inner_call(): pl.pallas_call(settle_inner_kernel, in_specs=[pl.BlockSpec(memory_space=p...]
    ppermute x2, waiting for transfers between devices: 0.01 us -> 2.18 us  [swap(): return lax.ppermute(v, axis, pairs + [(j, i) for i, j in pairs])]
    pallas_call x1, Pallas kernels: 4.12 us -> 2.02 us  [settle_call(): pl.pallas_call(settle_kernel, in_specs=[pl.BlockSpec(memory_space=pltpu.S...]
    pallas_call x1, Pallas kernels: 2.85 us -> 1.74 us  [advance_call(): pl.pallas_call(advance_kernel, in_specs=[pl.BlockSpec(memory_space=pltpu....]
    ppermute x2, starting transfers between devices: 5.38 us -> 4.56 us  [swap(): return lax.ppermute(v, axis, pairs + [(j, i) for i, j in pairs])]
    unnamed x4 -> x2, local copies, waits for them, and re-layouts: 0.76 us -> 0.01 us
  transfers between devices with their start and end apart: 6 -> 8, of which waited for: 2 -> 3; matrix products, arithmetic and copies ran while one was open for 0% -> 0% of each run, Pallas kernels for 39% -> 22%
where the time goes in v1:
time: 39.1 us; the launch traced here: 38.6 us
  Pallas kernels  20.1 us (51%)
  starting transfers between devices  11.3 us (29%)
  waiting for transfers between devices  6.34 us (16%)
  between operations  0.74 us (2%)
    ppermute x6, starting transfers between devices, ring(): return lax.ppermute(v, axis, [(i, (i + shift) % n) for i in range(n)])  6.71 us
    pallas_call x1, Pallas kernels, column_call(): pl.pallas_call(column_kernel, in_specs=[pl.BlockSpec(memory_space=pltpu.S...  5.71 us
    ppermute x2, starting transfers between devices, swap(): return lax.ppermute(v, axis, pairs + [(j, i) for i, j in pairs])  4.56 us
    ppermute x6, waiting for transfers between devices, ring(): return lax.ppermute(v, axis, [(i, (i + shift) % n) for i in range(n)])  4.16 us
    pallas_call x2, Pallas kernels, advance_inner_call(): pl.pallas_call(functools.partial(advance_inner_kernel, low, high), in_spe...  3.71 us
    pallas_call x1, Pallas kernels, settle_inner_call(): pl.pallas_call(settle_inner_kernel, in_specs=[pl.BlockSpec(memory_space=p...  3.22 us
    pallas_call x1, Pallas kernels, collide_call(): pl.pallas_call(collide_kernel, in_specs=[vmem, vmem], out_specs=[vmem, vm...  2.28 us
    ppermute x2, waiting for transfers between devices, swap(): return lax.ppermute(v, axis, pairs + [(j, i) for i, j in pairs])  2.18 us
  transfers between devices with their start and end apart: 8, of which 3 were waited for; matrix products, arithmetic and copies ran while one was open for 0% of the time, Pallas kernels for 22%

profile of v1, /device:TPU:1, one launch (start us, length us, event | category | flops | bytes accessed | tf_op | source)
XLA Modules:
  0.0 38.6 jit_solution(5268868149600447536)
XLA Ops:
  0.6 0.1 stack.23
  0.8 5.7 %columns.1 = (f32[7,32,128]{2,1,0:T(8,128)S(1)}, f32[8,26,32,256]{3,2,1,0:T(8,128)S(1)}, s32[8,32,256]{2,1,0:T(8,128)S(1)}) custom-call(s32[5]{0:T(128)S(1)} %convert_element_type.3.place, f32[19,32,8,256]{3,2,1,0:T(8,128)} %fluid.1, f32[7,32,8,256]{3,2,1,0:T(8,128)} %heat.1, s32[32,8,256]{2,1,0:T(8,128)} %mask.1, s32[32,256]{1,0:T(8,128)} %kind.5), custom_call_target="tpu_custom_call" | custom-call | flops 39321600 | bytes 13631488 | tf_op jit(solution)/shard_map/columns/pallas_call | solution.py:227
  6.5 2.3 %collide.1 = (f32[8,26,32,256]{3,2,1,0:T(8,128)S(1)}, f32[14,32,128]{2,1,0:T(8,128)S(1)}, f32[14,32,128]{2,1,0:T(8,128)S(1)}) custom-call(f32[8,26,32,256]{3,2,1,0:T(8,128)S(1)} %get-tuple-element.18.before, s32[8,32,256]{2,1,0:T(8,128)S(1)} %get-tuple-element.19.solid), custom_call_target="tpu_custom_call" | custom-call | flops 39321600 | bytes 13631488 | tf_op jit(solution)/shard_map/collide/pallas_call | solution.py:157
  8.8 2.6 %collective-permute-start.2 = (f32[14,32,128]{2,1,0:T(8,128)S(1)}, f32[14,32,128]{2,1,0:T(8,128)S(1)}, u32[]{:S(2)}, u32[]{:S(2)}) collective-permute-start(f32[14,32,128]{2,1,0:T(8,128)S(1)} %get-tuple-element.24), channel_id=1, source_target_pairs={{0,4},{4,8},{8,12},{12,16},{16,20},{20,24},{24,28},{28,0},{1,5},{5... | collective-permute-start | bytes 688136 | tf_op jit(solution)/shard_map/ppermute | solution.py:658
  11.4 0.0 collective-permute-start.3
  11.4 0.7 %collective-permute-start.1 = (f32[7,32,128]{2,1,0:T(8,128)S(1)}, f32[7,32,128]{2,1,0:T(8,128)S(1)}, u32[]{:S(2)}, u32[]{:S(2)}) collective-permute-start(f32[7,32,128]{2,1,0:T(8,128)S(1)} %get-tuple-element.21.own), channel_id=1, source_target_pairs={{1,2},{2,1},{5,6},{6,5},{9,10},{10,9},{13,14},{14,13},{17,18},{18,... | collective-permute-start | bytes 344072 | tf_op jit(solution)/shard_map/ppermute | solution.py:664
  12.1 3.9 %collective-permute-start = (f32[7,32,128]{2,1,0:T(8,128)S(1)}, f32[7,32,128]{2,1,0:T(8,128)S(1)}, u32[]{:S(2)}, u32[]{:S(2)}) collective-permute-start(f32[7,32,128]{2,1,0:T(8,128)S(1)} %get-tuple-element.21.own), channel_id=1, source_target_pairs={{0,1},{2,3},{1,0},{3,2},{4,5},{6,7},{5,4},{7,6},{8,9},{10,11},{9,8... | collective-permute-start | bytes 344072 | tf_op jit(solution)/shard_map/ppermute | solution.py:664
  16.0 0.0 collective-permute-done.1.odd
  16.0 2.2 %collective-permute-done.even = f32[7,32,128]{2,1,0:T(8,128)S(1)} collective-permute-done((f32[7,32,128]{2,1,0:T(8,128)S(1)}, f32[7,32,128]{2,1,0:T(8,128)S(1)}, u32[]{:S(2)}, u32[]{:S(2)}) %collective-permute-start) | collective-permute-done | bytes 114720 | tf_op jit(solution)/shard_map/ppermute | solution.py:664
  18.2 1.5 %strips.1 = (f32[28,32,128]{2,1,0:T(8,128)S(1)}, f32[32,128]{1,0:T(8,128)S(1)}, f32[32,128]{1,0:T(8,128)S(1)}) custom-call(s32[5]{0:T(128)S(1)} %convert_element_type.3.place, f32[7,32,128]{2,1,0:T(8,128)S(1)} %get-tuple-element.21.own, f32[7,32,128]{2,1,0:T(8,128)S(1)} %collective-permute-done.even, f32[7,32,128]{2,1,0:T(8,128)S(1)} %collective-permute-done.1.odd, ...), custom_call_target="tpu_custom_call" | custom-call | tf_op jit(solution)/shard_map/strips/pallas_call | solution.py:312
  19.6 3.1 %collective-permute-start.4 = (f32[32,128]{1,0:T(8,128)S(1)}, f32[32,128]{1,0:T(8,128)S(1)}, u32[]{:S(2)}, u32[]{:S(2)}) collective-permute-start(f32[32,128]{1,0:T(8,128)S(1)} %get-tuple-element.25), channel_id=1, source_target_pairs={{0,4},{4,8},{8,12},{12,16},{16,20},{20,24},{24,28},{28,0},{1,5},{5... | collective-permute-start | bytes 49160 | tf_op jit(solution)/shard_map/ppermute | solution.py:658
  22.7 0.0 collective-permute-start.5
  22.7 0.0 copy-start
  22.7 1.9 %advance_inner.2.next_in = f32[8,26,32,256]{3,2,1,0:T(8,128)S(1)} custom-call(s32[5]{0:T(128)S(1)} %convert_element_type.3.place, f32[8,26,32,256]{3,2,1,0:T(8,128)S(1)} %get-tuple-element.20.post, f32[28,32,128]{2,1,0:T(8,128)S(1)} %get-tuple-element.23.strip.strip_in), custom_call_target="tpu_custom_call" | custom-call | flops 29491200 | bytes 10223616 | tf_op jit(solution)/shard_map/advance_inner/pallas_call | solution.py:420
  24.6 0.0 collective-permute-done.4.strip_w
  24.6 1.5 %collective-permute-done.5.strip_e = f32[32,128]{1,0:T(8,128)S(1)} collective-permute-done((f32[32,128]{1,0:T(8,128)S(1)}, f32[32,128]{1,0:T(8,128)S(1)}, u32[]{:S(2)}, u32[]{:S(2)}) %collective-permute-start.5) | collective-permute-done | bytes 16416 | tf_op jit(solution)/shard_map/ppermute | solution.py:658
  26.0 0.0 collective-permute-done.2.west
  26.0 0.0 collective-permute-done.3.east
  26.0 0.0 copy-done
  26.1 1.7 %advance.1 = (f32[8,26,32,256]{3,2,1,0:T(8,128)S(1)}, f32[26,32,128]{2,1,0:T(8,128)S(1)}, f32[13,32,128]{2,1,0:T(8,128)S(1)}, f32[13,32,128]{2,1,0:T(8,128)S(1)}, f32[6,32,128]{2,1,0:T(8,128)S(1)}) custom-call(s32[5]{0:T(128)S(1)} %convert_element_type.3.place, f32[8,26,32,256]{3,2,1,0:T(8,128)S(1)} %get-tuple-element.20.post, ...), custom_call_target="tpu_custom_call", output_to_operand_aliasing={{0}: (8, {})} | custom-call | flops 14745600 | bytes 5111808 | tf_op jit(solution)/shard_map/advance/pallas_call | solution.py:505
  27.8 0.4 collective-permute-start.6
  28.2 0.6 %collective-permute-start.7 = (f32[13,32,128]{2,1,0:T(8,128)S(1)}, f32[13,32,128]{2,1,0:T(8,128)S(1)}, u32[]{:S(2)}, u32[]{:S(2)}) collective-permute-start(f32[13,32,128]{2,1,0:T(8,128)S(1)} %get-tuple-element.29), channel_id=1, source_target_pairs={{0,28},{4,0},{8,4},{12,8},{16,12},{20,16},{24,20},{28,24},{1,29},{... | collective-permute-start | bytes 638984 | tf_op jit(solution)/shard_map/ppermute | solution.py:658
  28.8 1.9 %advance_inner.3.post = f32[8,26,32,256]{3,2,1,0:T(8,128)S(1)} custom-call(s32[5]{0:T(128)S(1)} %convert_element_type.3.place, f32[8,26,32,256]{3,2,1,0:T(8,128)S(1)} %get-tuple-element.20.post, f32[28,32,128]{2,1,0:T(8,128)S(1)} %get-tuple-element.23.strip.strip_in, f32[8,26,32,256]{3,2,1,0:T(8,128)S(1)} %get-tuple-element.27.refs_0_), custom_call_target="tpu_custom_call", output_to_operand_aliasing={{}: (3, {})} | custom-call | flops 29491200 | bytes 10223616 | tf_op jit(solution)/shard_map/advance_inner/pallas_call | solution.py:420
  30.7 3.2 %settle_inner.1 = (f32[19,32,8,256]{3,2,1,0:T(8,128)}, f32[7,32,8,256]{3,2,1,0:T(8,128)}) custom-call(s32[5]{0:T(128)S(1)} %convert_element_type.3.place, f32[8,26,32,256]{3,2,1,0:T(8,128)S(1)} %get-tuple-element.18.before, f32[8,26,32,256]{3,2,1,0:T(8,128)S(1)} %advance_inner.3.post, f32[26,32,128]{2,1,0:T(8,128)S(1)} %get-tuple-element.30.strip.strip_in), custom_call_target="tpu_custom_call" | custom-call | flops 58982400 | bytes 20447232 | tf_op jit(solution)/shard_map/settle_inner/pallas_call | solution.py:581
  33.9 0.0 collective-permute-done.6.west
  33.9 2.7 %collective-permute-done.7.east = f32[13,32,128]{2,1,0:T(8,128)S(1)} collective-permute-done((f32[13,32,128]{2,1,0:T(8,128)S(1)}, f32[13,32,128]{2,1,0:T(8,128)S(1)}, u32[]{:S(2)}, u32[]{:S(2)}) %collective-permute-start.7) | collective-permute-done | bytes 213024 | tf_op jit(solution)/shard_map/ppermute | solution.py:658
  36.6 2.0 %settle.1 = (f32[19,32,8,256]{3,2,1,0:T(8,128)}, f32[7,32,8,256]{3,2,1,0:T(8,128)}) custom-call(s32[5]{0:T(128)S(1)} %convert_element_type.3.place, f32[8,26,32,256]{3,2,1,0:T(8,128)S(1)} %get-tuple-element.18.before, f32[8,26,32,256]{3,2,1,0:T(8,128)S(1)} %advance_inner.3.post, ...), custom_call_target="tpu_custom_call", output_to_operand_aliasing={{0}: (8, {}), {1}: (9, {})} | custom-call | flops 14745600 | bytes 5111808 | tf_op jit(solution)/shard_map/settle/pallas_call | solution.py:638
  (1 shorter events, 0.0 us)
Async XLA Ops:
  8.8 17.3 %collective-permute-start.2 = (f32[14,32,128]{2,1,0:T(8,128)S(1)}, f32[14,32,128]{2,1,0:T(8,128)S(1)}, u32[]{:S(2)}, u32[]{:S(2)}) collective-permute-start(f32[14,32,128]{2,1,0:T(8,128)S(1)} %get-tuple-element.24), channel_id=1, source_target_pairs={{0,4},{4,8},{8,12},{12,16},{16,20},{20,24},{24,28},{28,0},{1,5},{5... | collective-permute-start | bytes 688136 | tf_op jit(solution)/shard_map/ppermute | solution.py:658
  11.4 14.6 %collective-permute-start.3 = (f32[14,32,128]{2,1,0:T(8,128)S(1)}, f32[14,32,128]{2,1,0:T(8,128)S(1)}, u32[]{:S(2)}, u32[]{:S(2)}) collective-permute-start(f32[14,32,128]{2,1,0:T(8,128)S(1)} %get-tuple-element.22.after), channel_id=1, source_target_pairs={{0,28},{4,0},{8,4},{12,8},{16,12},{20,16},{24,20},{28,24},{1,29},{... | collective-permute-start | bytes 688136 | tf_op jit(solution)/shard_map/ppermute | solution.py:658
  11.4 4.6 %collective-permute-start.1 = (f32[7,32,128]{2,1,0:T(8,128)S(1)}, f32[7,32,128]{2,1,0:T(8,128)S(1)}, u32[]{:S(2)}, u32[]{:S(2)}) collective-permute-start(f32[7,32,128]{2,1,0:T(8,128)S(1)} %get-tuple-element.21.own), channel_id=1, source_target_pairs={{1,2},{2,1},{5,6},{6,5},{9,10},{10,9},{13,14},{14,13},{17,18},{18,... | collective-permute-start | bytes 344072 | tf_op jit(solution)/shard_map/ppermute | solution.py:664
  12.1 6.1 %collective-permute-start = (f32[7,32,128]{2,1,0:T(8,128)S(1)}, f32[7,32,128]{2,1,0:T(8,128)S(1)}, u32[]{:S(2)}, u32[]{:S(2)}) collective-permute-start(f32[7,32,128]{2,1,0:T(8,128)S(1)} %get-tuple-element.21.own), channel_id=1, source_target_pairs={{0,1},{2,3},{1,0},{3,2},{4,5},{6,7},{5,4},{7,6},{8,9},{10,11},{9,8... | collective-permute-start | bytes 344072 | tf_op jit(solution)/shard_map/ppermute | solution.py:664
  19.6 4.9 %collective-permute-start.4 = (f32[32,128]{1,0:T(8,128)S(1)}, f32[32,128]{1,0:T(8,128)S(1)}, u32[]{:S(2)}, u32[]{:S(2)}) collective-permute-start(f32[32,128]{1,0:T(8,128)S(1)} %get-tuple-element.25), channel_id=1, source_target_pairs={{0,4},{4,8},{8,12},{12,16},{16,20},{20,24},{24,28},{28,0},{1,5},{5... | collective-permute-start | bytes 49160 | tf_op jit(solution)/shard_map/ppermute | solution.py:658
  22.7 3.3 %collective-permute-start.5 = (f32[32,128]{1,0:T(8,128)S(1)}, f32[32,128]{1,0:T(8,128)S(1)}, u32[]{:S(2)}, u32[]{:S(2)}) collective-permute-start(f32[32,128]{1,0:T(8,128)S(1)} %get-tuple-element.26), channel_id=1, source_target_pairs={{0,28},{4,0},{8,4},{12,8},{16,12},{20,16},{24,20},{28,24},{1,29},{... | collective-permute-start | bytes 49160 | tf_op jit(solution)/shard_map/ppermute | solution.py:658
  22.7 3.4 %copy-start = (s32[32,256]{1,0:T(8,128)S(1)}, s32[32,256]{1,0:T(8,128)}, u32[]{:S(2)}) copy-start(s32[32,256]{1,0:T(8,128)} %kind.5) | copy-start | bytes 98308
  27.8 6.1 %collective-permute-start.6 = (f32[13,32,128]{2,1,0:T(8,128)S(1)}, f32[13,32,128]{2,1,0:T(8,128)S(1)}, u32[]{:S(2)}, u32[]{:S(2)}) collective-permute-start(f32[13,32,128]{2,1,0:T(8,128)S(1)} %get-tuple-element.28), channel_id=1, source_target_pairs={{0,4},{4,8},{8,12},{12,16},{16,20},{20,24},{24,28},{28,0},{1,5},{5... | collective-permute-start | bytes 638984 | tf_op jit(solution)/shard_map/ppermute | solution.py:658
  28.2 8.4 %collective-permute-start.7 = (f32[13,32,128]{2,1,0:T(8,128)S(1)}, f32[13,32,128]{2,1,0:T(8,128)S(1)}, u32[]{:S(2)}, u32[]{:S(2)}) collective-permute-start(f32[13,32,128]{2,1,0:T(8,128)S(1)} %get-tuple-element.29), channel_id=1, source_target_pairs={{0,28},{4,0},{8,4},{12,8},{16,12},{20,16},{24,20},{28,24},{1,29},{... | collective-permute-start | bytes 638984 | tf_op jit(solution)/shard_map/ppermute | solution.py:658
